TPU v7x, 32 devices: a whole 2x2x4 slice. The times are simulated.
32 devices in a mesh: tm: 16 (over z, y, x), row: 2 (over core).
Axes of the slice: x: 2, y: 2, z: 4, core: 2. Of those that a mesh axis runs over, the one named last changes fastest.
Arguments:
- initial: float32 [1024], replicated, may hold values from -6 to 6
- dynamics: float32 [1024, 1024], replicated, may hold values from -0.009765625 to 0.009765625
- obs_rows: bfloat16 [32768, 1024], P('tm', 'row'), may hold values from -0.1875 to 0.1875
- obs_values: bfloat16 [32768], P('tm'), may hold values from -6 to 6
- obs_slab: int32 [32768, 1], P('tm'), may hold values from 0 to 31; in each aligned block of 2048 rows (0 to 2047, 2048 to 4095, ...) at most 64 rows name the same one
Outputs:
- states: float32 [32, 1024], P('tm', 'row')
Inputs may be any that keep to these rules, and one draw needn't show every extreme that they name: `obs_slab`: within the rows ingested by one index of tm, no slab is named by more than 64 rows, a bound that some block reaches of them.
All inputs are finite; a program needn't handle non-finite values.
Results may differ from a plain program's by a relative error of at most 0.0003.
Values may be sent and summed in bfloat16 or wider, within the bound.
A program may use at most 128 MiB of HBM per device.

v0:
```python
import jax
import jax.numpy as jnp
from jax import lax
from jax.sharding import PartitionSpec as P

SLAB_DEV = 2
CAP = 64


sigma_gain = 0.3


def shifted(value, axis, steps):
    count = lax.axis_size(axis)
    first, last = (max(0, -steps), min(count, count - steps))
    return lax.ppermute(value, axis, [(source, source + steps) for source in range(first, last)])


def left_product(left_rows, pieces):
    new_matrix = jnp.dot(left_rows, pieces[0], precision=lax.Precision.HIGHEST)
    new_vector = jnp.dot(left_rows, pieces[1], precision=lax.Precision.HIGHEST)
    return (new_matrix, new_vector)


def body(initial, dynamics, obs_rows, obs_values, obs_slab):
    time_devs = lax.axis_size("tm")
    row_devs = lax.axis_size("row")
    state_width = dynamics.shape[1]
    local_cols = state_width // row_devs
    row_start = lax.axis_index("row") * local_cols
    time_index = lax.axis_index("tm")
    capacity = CAP
    slab_total = SLAB_DEV * time_devs
    obs_count = obs_rows.shape[0]
    target = obs_slab[:, 0]
    onehot = (target[:, None] == jnp.arange(slab_total, dtype=jnp.int32)[None, :]).astype(jnp.int32)
    rank_in = jnp.sum(onehot * (jnp.cumsum(onehot, axis=0) - 1), axis=1)
    owner_dev = target // SLAB_DEV
    within = target % SLAB_DEV
    slot_index = (within * time_devs + owner_dev) * capacity + rank_in
    slot_table = (
        jnp.full((slab_total * capacity,), obs_count, jnp.int32)
        .at[slot_index]
        .set(jnp.arange(obs_count, dtype=jnp.int32))
    )
    padded_rows = jnp.concatenate([obs_rows, jnp.zeros((1, local_cols), jnp.bfloat16)], axis=0)
    padded_values = jnp.concatenate([obs_values, jnp.zeros((1,), jnp.bfloat16)], axis=0)
    send_rows = padded_rows[slot_table].reshape(SLAB_DEV, time_devs, capacity, local_cols)
    send_values = padded_values[slot_table].reshape(SLAB_DEV, time_devs, capacity)
    recv_rows, recv_values = (
        lax.all_to_all(send_rows, "tm", split_axis=1, concat_axis=1, tiled=True),
        lax.all_to_all(send_values, "tm", split_axis=1, concat_axis=1, tiled=True),
    )
    slab_rows = recv_rows.reshape(SLAB_DEV, time_devs * capacity, local_cols)
    slab_values = recv_values.reshape(SLAB_DEV, time_devs * capacity)
    information = jnp.einsum(
        "sra,srb->sab",
        slab_rows,
        lax.all_gather(slab_rows, "row", axis=2, tiled=True),
        preferred_element_type=jnp.float32,
    )
    moment = jnp.einsum("sr,sra->sa", slab_values, slab_rows, preferred_element_type=jnp.float32)
    evolve = jnp.eye(state_width, dtype=jnp.float32) + dynamics
    evolve_rows = lax.dynamic_slice_in_dim(evolve, row_start, local_cols, 0)
    transitions = []
    offsets = []
    for slab_index in range(SLAB_DEV):
        transitions.append(
            evolve_rows
            - sigma_gain * jnp.dot(information[slab_index], evolve, precision=lax.Precision.HIGHEST)
        )
        offsets.append(sigma_gain * moment[slab_index])
    composed = transitions[0]
    composed_offset = offsets[0]
    slab_index = 1
    new_matrix, new_vector = left_product(
        transitions[slab_index],
        (
            lax.all_gather(composed, "row", axis=0, tiled=True),
            lax.all_gather(composed_offset, "row", axis=0, tiled=True),
        ),
    )
    composed = new_matrix
    composed_offset = new_vector + offsets[slab_index]
    initial_rows = lax.dynamic_slice_in_dim(initial, row_start, local_cols, 0)

    def advance(turn, state_rows):
        whole_state = lax.all_gather(state_rows, "row", axis=0, tiled=True)
        leaving = jnp.dot(composed, whole_state, precision=lax.Precision.HIGHEST) + composed_offset
        arriving = shifted(leaving, "tm", 1)
        return jnp.where(time_index == 0, initial_rows, arriving)

    entry_rows = lax.fori_loop(0, time_devs - 1, advance, initial_rows)
    states = []
    current = entry_rows
    for slab_index in range(SLAB_DEV):
        whole_state = lax.all_gather(current, "row", axis=0, tiled=True)
        current = (
            jnp.dot(transitions[slab_index], whole_state, precision=lax.Precision.HIGHEST)
            + offsets[slab_index]
        )
        states.append(current)
    return jnp.stack(states)


def solution(mesh):
    placed = (P(), P(), P("tm", "row"), P("tm"), P("tm", None))
    return jax.shard_map(
        body, mesh=mesh, in_specs=placed, out_specs=P("tm", "row"), check_vma=False
    )
```

profile of v0, /device:TPU:9, one launch (start us, length us, event | category | flops | bytes accessed | tf_op | source)
XLA Modules:
  0.0 357.0 jit_solution(5598932367776925572)
XLA Ops:
  7.3 9.1 %reduce-window.6 = s32[32,16,128]{2,1,0:T(8,128)S(1)} reduce-window(s32[32,16,128]{2,1,0:T(8,128)S(1)} %fusion.4, s32[]{:T(128)} %copy.37), window={size=1x1x128 pad=0_0x0_0x127_0}, to_apply=%region_0.0 | reduce-window | flops 8323072 | bytes 524292 | tf_op jit(solution)/shard_map/reduce-window
  17.3 8.0 %scatter_custom_fusion = s32[2048]{0:T(1024)S(1)} fusion(s32[2048]{0:T(1024)S(1)} %bitcast.110, s32[2048]{0:T(1024)S(1)} %iota.23, s32[]{:T(128)} %constant.63.clone.1), kind=kCustom, calls=%fused_computation.34 | custom fusion | bytes 8196 | tf_op jit(solution)/shard_map/scatter | solution.py:44
  27.1 9.2 %gather_fusion = bf16[2048,512]{1,0:T(8,128)(2,1)} fusion(bf16[2049,512]{1,0:T(8,128)(2,1)S(1)} %concatenate.6, s32[2048]{0:T(1024)S(1)} %fusion.5), kind=kCustom, calls=%fused_computation | custom fusion | bytes 4202496 | tf_op jit(solution)/shard_map/gather | solution.py:48
  38.2 53.8 %all_to_all.10 = bf16[2,16,64,512]{3,2,0,1:T(8,128)(2,1)S(1)} all-to-all(bf16[2,16,64,512]{3,2,0,1:T(8,128)(2,1)S(1)} %copy.17), channel_id=1, replica_groups=mesh['tm'=16,'row'=2] {'tm'}, dimensions={1} | all-to-all | bytes 4194304 | tf_op jit(solution)/shard_map/all_to_all | solution.py:51
  93.7 5.0 %convert_add_fusion = f32[1024,1024]{1,0:T(8,128)} fusion(f32[1024,1024]{1,0:T(8,128)} %param.8), kind=kLoop, calls=%fused_computation.4 | loop fusion | flops 3145728 | bytes 8388608 | tf_op jit(solution)/shard_map/add | solution.py:63
  98.6 9.4 %all-gather.9.cloned.1.call-done = bf16[2,1024,1024]{2,1,0:T(8,128)(2,1)} async-done(((bf16[2,1024,512]{2,1,0:T(8,128)(2,1)}), bf16[2,1024,1024]{2,1,0:T(8,128)(2,1)}) %all-gather.9.cloned.1.call-update) | async-done | bytes 4194320 | tf_op jit(solution)/shard_map/all_gather | solution.py:59
  108.0 4.7 %fusion.13 = f32[2,512,1024]{2,1,0:T(8,128)S(1)} fusion(bf16[2,1024,512]{2,1,0:T(8,128)(2,1)S(1)} %bitcast.86, bf16[2,1024,1024]{2,1,0:T(8,128)(2,1)} %all-gather.9.cloned.1.call-done), kind=kOutput, calls=%fused_computation.39 | convolution fusion | flops 2147483648 | bytes 10485760 | tf_op jit(solution)/shard_map/sra,srb->sab/dot_general | solution.py:56
  112.8 1.9 copy-done.4
  114.7 8.2 %multiply_subtract_fusion.1 = f32[512,1024]{1,0:T(8,128)} fusion(f32[1024,1024]{1,0:T(8,128)S(1)} %copy-done, s32[]{:T(128)S(6)} %select_n.38, f32[2,512,1024]{2,1,0:T(8,128)S(1)} %fusion.13), kind=kOutput, calls=%fused_computation.11 | convolution fusion | flops 6443499520 | bytes 10485764 | tf_op jit(solution)/shard_map/dot_general | solution.py:70
  123.6 13.1 %gather_fusion.1 = bf16[2048]{0:T(1024)(128)(2,1)S(1)} fusion(bf16[2049]{0:T(1024)(128)(2,1)S(1)} %pad_maximum_fusion, s32[2048]{0:T(1024)S(1)} %fusion.5), kind=kCustom, calls=%fused_computation.1 | custom fusion | bytes 16384 | tf_op jit(solution)/shard_map/gather | solution.py:49
  137.4 6.4 %all-to-all-start.1 = ((bf16[2,16,64]{2,0,1:T(2,128)(2,1)}), bf16[2,16,64]{2,0,1:T(2,128)(2,1)S(1)}, u32[]{:S(2)}, u32[]{:S(2)}) async-start(bf16[2,16,64]{2,0,1:T(2,128)(2,1)} %copy.20), calls=%async_computation.1 | async-start | bytes 16384 | tf_op jit(solution)/shard_map/all_to_all | solution.py:52
  143.9 5.0 %all-to-all-done.1 = bf16[2,16,64]{2,0,1:T(2,128)(2,1)S(1)} async-done(((bf16[2,16,64]{2,0,1:T(2,128)(2,1)}), bf16[2,16,64]{2,0,1:T(2,128)(2,1)S(1)}, u32[]{:S(2)}, u32[]{:S(2)}) %all-to-all-start.1) | async-done | bytes 4128 | tf_op jit(solution)/shard_map/all_to_all | solution.py:52
  149.4 3.1 all-gather
  152.5 10.1 %multiply_subtract_fusion = f32[512,1024]{1,0:T(8,128)S(1)} fusion(f32[1024,1024]{1,0:T(8,128)} %convert_add_fusion, s32[]{:T(128)S(6)} %select_n.38, f32[2,512,1024]{2,1,0:T(8,128)} %copy-done.4), kind=kOutput, calls=%fused_computation.10 | convolution fusion | flops 6443499520 | bytes 10485764 | tf_op jit(solution)/shard_map/dot_general | solution.py:70
  164.0 1.9 fusion.8
  165.9 9.7 %fusion.14 = f32[512,1024]{1,0:T(8,128)S(1)} fusion(f32[512,1024]{1,0:T(8,128)} %copy-done.1, f32[1024,1024]{1,0:T(8,128)} %all-gather.11.cloned.1.call-done), kind=kOutput, calls=%fused_computation.40 | convolution fusion | flops 6442450944 | bytes 8388608 | tf_op jit(solution)/shard_map/dot_general | solution.py:20
  175.6 163.7 %while.12 = (s32[]{:T(128)}, f32[512]{0:T(512)S(1)}, pred[]{:T(512)}, f32[512,1024]{1,0:T(8,128)S(1)}, f32[512]{0:T(512)S(1)}, /*index=5*/f32[512]{0:T(512)S(1)}, s32[]{:T(128)}) while((s32[]{:T(128)}, f32[512]{0:T(512)S(1)}, pred[]{:T(512)}, f32[512,1024]{1,0:T(8,128)S(1)}, f32[512]{0:T(512)S(1)}, /*index=5*/f32[512]{0:T(512)S(1)}, ...), condition=%wide.region_5.6_spmd, body=%wide.region_4.5_spmd.sunk | while | flops 6292482 | bytes 2130038 | solution.py:93
  179.3 2.2 collective-permute-start
  181.5 3.9 %collective-permute-done = f32[512]{0:T(512)S(1)} collective-permute-done((f32[512]{0:T(512)S(1)}, f32[512]{0:T(512)S(1)}, u32[]{:S(2)}, u32[]{:S(2)}) %collective-permute-start) | collective-permute-done | bytes 2080 | tf_op jit(solution)/shard_map/while/body/eval_jaxpr/ppermute | solution.py:16
  185.4 3.0 all-gather.5
  190.3 1.9 collective-permute-start
  192.2 4.2 %collective-permute-done = f32[512]{0:T(512)S(1)} collective-permute-done((f32[512]{0:T(512)S(1)}, f32[512]{0:T(512)S(1)}, u32[]{:S(2)}, u32[]{:S(2)}) %collective-permute-start) | collective-permute-done | bytes 2080 | tf_op jit(solution)/shard_map/while/body/eval_jaxpr/ppermute | solution.py:16
  196.4 3.0 all-gather.5
  201.3 1.9 collective-permute-start
  203.2 4.2 %collective-permute-done = f32[512]{0:T(512)S(1)} collective-permute-done((f32[512]{0:T(512)S(1)}, f32[512]{0:T(512)S(1)}, u32[]{:S(2)}, u32[]{:S(2)}) %collective-permute-start) | collective-permute-done | bytes 2080 | tf_op jit(solution)/shard_map/while/body/eval_jaxpr/ppermute | solution.py:16
  207.4 3.0 all-gather.5
  212.2 1.9 collective-permute-start
  214.2 4.2 %collective-permute-done = f32[512]{0:T(512)S(1)} collective-permute-done((f32[512]{0:T(512)S(1)}, f32[512]{0:T(512)S(1)}, u32[]{:S(2)}, u32[]{:S(2)}) %collective-permute-start) | collective-permute-done | bytes 2080 | tf_op jit(solution)/shard_map/while/body/eval_jaxpr/ppermute | solution.py:16
  218.4 3.0 all-gather.5
  223.2 1.9 collective-permute-start
  225.2 4.2 %collective-permute-done = f32[512]{0:T(512)S(1)} collective-permute-done((f32[512]{0:T(512)S(1)}, f32[512]{0:T(512)S(1)}, u32[]{:S(2)}, u32[]{:S(2)}) %collective-permute-start) | collective-permute-done | bytes 2080 | tf_op jit(solution)/shard_map/while/body/eval_jaxpr/ppermute | solution.py:16
  229.4 3.0 all-gather.5
  234.2 1.9 collective-permute-start
  236.2 4.2 %collective-permute-done = f32[512]{0:T(512)S(1)} collective-permute-done((f32[512]{0:T(512)S(1)}, f32[512]{0:T(512)S(1)}, u32[]{:S(2)}, u32[]{:S(2)}) %collective-permute-start) | collective-permute-done | bytes 2080 | tf_op jit(solution)/shard_map/while/body/eval_jaxpr/ppermute | solution.py:16
  240.4 3.0 all-gather.5
  245.2 1.9 collective-permute-start
  247.1 4.2 %collective-permute-done = f32[512]{0:T(512)S(1)} collective-permute-done((f32[512]{0:T(512)S(1)}, f32[512]{0:T(512)S(1)}, u32[]{:S(2)}, u32[]{:S(2)}) %collective-permute-start) | collective-permute-done | bytes 2080 | tf_op jit(solution)/shard_map/while/body/eval_jaxpr/ppermute | solution.py:16
  251.3 3.0 all-gather.5
  256.2 1.9 collective-permute-start
  258.1 4.2 %collective-permute-done = f32[512]{0:T(512)S(1)} collective-permute-done((f32[512]{0:T(512)S(1)}, f32[512]{0:T(512)S(1)}, u32[]{:S(2)}, u32[]{:S(2)}) %collective-permute-start) | collective-permute-done | bytes 2080 | tf_op jit(solution)/shard_map/while/body/eval_jaxpr/ppermute | solution.py:16
  262.3 3.0 all-gather.5
  267.2 1.9 collective-permute-start
  269.1 4.2 %collective-permute-done = f32[512]{0:T(512)S(1)} collective-permute-done((f32[512]{0:T(512)S(1)}, f32[512]{0:T(512)S(1)}, u32[]{:S(2)}, u32[]{:S(2)}) %collective-permute-start) | collective-permute-done | bytes 2080 | tf_op jit(solution)/shard_map/while/body/eval_jaxpr/ppermute | solution.py:16
  273.3 3.0 all-gather.5
  278.2 1.9 collective-permute-start
  280.1 4.2 %collective-permute-done = f32[512]{0:T(512)S(1)} collective-permute-done((f32[512]{0:T(512)S(1)}, f32[512]{0:T(512)S(1)}, u32[]{:S(2)}, u32[]{:S(2)}) %collective-permute-start) | collective-permute-done | bytes 2080 | tf_op jit(solution)/shard_map/while/body/eval_jaxpr/ppermute | solution.py:16
  284.3 3.0 all-gather.5
  289.1 1.9 collective-permute-start
  291.1 4.2 %collective-permute-done = f32[512]{0:T(512)S(1)} collective-permute-done((f32[512]{0:T(512)S(1)}, f32[512]{0:T(512)S(1)}, u32[]{:S(2)}, u32[]{:S(2)}) %collective-permute-start) | collective-permute-done | bytes 2080 | tf_op jit(solution)/shard_map/while/body/eval_jaxpr/ppermute | solution.py:16
  295.3 3.0 all-gather.5
  300.1 1.9 collective-permute-start
  302.1 4.2 %collective-permute-done = f32[512]{0:T(512)S(1)} collective-permute-done((f32[512]{0:T(512)S(1)}, f32[512]{0:T(512)S(1)}, u32[]{:S(2)}, u32[]{:S(2)}) %collective-permute-start) | collective-permute-done | bytes 2080 | tf_op jit(solution)/shard_map/while/body/eval_jaxpr/ppermute | solution.py:16
  306.3 3.0 all-gather.5
  311.1 1.9 collective-permute-start
  313.1 4.2 %collective-permute-done = f32[512]{0:T(512)S(1)} collective-permute-done((f32[512]{0:T(512)S(1)}, f32[512]{0:T(512)S(1)}, u32[]{:S(2)}, u32[]{:S(2)}) %collective-permute-start) | collective-permute-done | bytes 2080 | tf_op jit(solution)/shard_map/while/body/eval_jaxpr/ppermute | solution.py:16
  317.3 3.0 all-gather.5
  322.1 1.9 collective-permute-start
  324.0 4.2 %collective-permute-done = f32[512]{0:T(512)S(1)} collective-permute-done((f32[512]{0:T(512)S(1)}, f32[512]{0:T(512)S(1)}, u32[]{:S(2)}, u32[]{:S(2)}) %collective-permute-start) | collective-permute-done | bytes 2080 | tf_op jit(solution)/shard_map/while/body/eval_jaxpr/ppermute | solution.py:16
  328.2 3.0 all-gather.5
  333.1 1.9 collective-permute-start
  335.0 4.2 %collective-permute-done = f32[512]{0:T(512)S(1)} collective-permute-done((f32[512]{0:T(512)S(1)}, f32[512]{0:T(512)S(1)}, u32[]{:S(2)}, u32[]{:S(2)}) %collective-permute-start) | collective-permute-done | bytes 2080 | tf_op jit(solution)/shard_map/while/body/eval_jaxpr/ppermute | solution.py:16
  339.2 3.1 all-gather.2
  342.3 3.4 fusion.16
  347.6 1.9 fusion.17
  (93 shorter events, 42.6 us)
Async XLA Ops:
  6.5 10.6 %copy-start.5 = (s32[2048,1]{0,1:T(1,128)S(1)}, s32[2048,1]{0,1:T(1,128)}, u32[]{:S(2)}) copy-start(s32[2048,1]{0,1:T(1,128)} %param.11) | copy-start | bytes 24580
  6.5 101.5 %all-gather.9.cloned.1.call-start = ((), (), s32[]{:S(2)}) async-start(), calls=%async_computation.2 | async-start | bytes 6291456 | tf_op jit(solution)/shard_map/all_gather | solution.py:59
  93.6 72.3 %all-gather.11.cloned.1.call-start = ((), (), s32[]{:S(2)}) async-start(), calls=%async_computation.3 | async-start | bytes 6291456 | tf_op jit(solution)/shard_map/all_gather | solution.py:79
  93.7 14.4 %copy-start.3 = (bf16[2,16,64,512]{3,2,1,0:T(8,128)(2,1)S(1)}, bf16[2,16,64,512]{3,2,1,0:T(8,128)(2,1)}, u32[]{:S(2)}) copy-start(bf16[2,16,64,512]{3,2,1,0:T(8,128)(2,1)} %copy.18) | copy-start | bytes 6291460
  108.0 6.7 %copy-start = (f32[1024,1024]{1,0:T(8,128)S(1)}, f32[1024,1024]{1,0:T(8,128)}, u32[]{:S(2)}) copy-start(f32[1024,1024]{1,0:T(8,128)} %convert_add_fusion) | copy-start | bytes 12582916
  112.7 2.0 copy-start.4
  123.0 0.7 copy-start.6
  123.6 20.2 %copy-start.7 = (f32[1024]{0:T(1024)S(1)}, f32[1024]{0:T(1024)}, u32[]{:S(2)}) copy-start(f32[1024]{0:T(1024)} %param.7) | copy-start | bytes 12292
  137.4 11.5 %all-to-all-start.1 = ((bf16[2,16,64]{2,0,1:T(2,128)(2,1)}), bf16[2,16,64]{2,0,1:T(2,128)(2,1)S(1)}, u32[]{:S(2)}, u32[]{:S(2)}) async-start(bf16[2,16,64]{2,0,1:T(2,128)(2,1)} %copy.20), calls=%async_computation.1 | async-start | bytes 16384 | tf_op jit(solution)/shard_map/all_to_all | solution.py:52
  162.7 1.3 copy-start.1
  179.3 6.1 %collective-permute-start = (f32[512]{0:T(512)S(1)}, f32[512]{0:T(512)S(1)}, u32[]{:S(2)}, u32[]{:S(2)}) collective-permute-start(f32[512]{0:T(512)S(1)} %add.85), channel_id=1, source_target_pairs={{0,2},{2,4},{4,6},{6,8},{8,10},{10,12},{12,14},{14,16},{16,18},{18... | collective-permute-start | bytes 6152 | tf_op jit(solution)/shard_map/while/body/eval_jaxpr/ppermute | solution.py:16
  190.3 6.1 %collective-permute-start = (f32[512]{0:T(512)S(1)}, f32[512]{0:T(512)S(1)}, u32[]{:S(2)}, u32[]{:S(2)}) collective-permute-start(f32[512]{0:T(512)S(1)} %add.85), channel_id=1, source_target_pairs={{0,2},{2,4},{4,6},{6,8},{8,10},{10,12},{12,14},{14,16},{16,18},{18... | collective-permute-start | bytes 6152 | tf_op jit(solution)/shard_map/while/body/eval_jaxpr/ppermute | solution.py:16
  201.3 6.1 %collective-permute-start = (f32[512]{0:T(512)S(1)}, f32[512]{0:T(512)S(1)}, u32[]{:S(2)}, u32[]{:S(2)}) collective-permute-start(f32[512]{0:T(512)S(1)} %add.85), channel_id=1, source_target_pairs={{0,2},{2,4},{4,6},{6,8},{8,10},{10,12},{12,14},{14,16},{16,18},{18... | collective-permute-start | bytes 6152 | tf_op jit(solution)/shard_map/while/body/eval_jaxpr/ppermute | solution.py:16
  212.2 6.1 %collective-permute-start = (f32[512]{0:T(512)S(1)}, f32[512]{0:T(512)S(1)}, u32[]{:S(2)}, u32[]{:S(2)}) collective-permute-start(f32[512]{0:T(512)S(1)} %add.85), channel_id=1, source_target_pairs={{0,2},{2,4},{4,6},{6,8},{8,10},{10,12},{12,14},{14,16},{16,18},{18... | collective-permute-start | bytes 6152 | tf_op jit(solution)/shard_map/while/body/eval_jaxpr/ppermute | solution.py:16
  223.2 6.1 %collective-permute-start = (f32[512]{0:T(512)S(1)}, f32[512]{0:T(512)S(1)}, u32[]{:S(2)}, u32[]{:S(2)}) collective-permute-start(f32[512]{0:T(512)S(1)} %add.85), channel_id=1, source_target_pairs={{0,2},{2,4},{4,6},{6,8},{8,10},{10,12},{12,14},{14,16},{16,18},{18... | collective-permute-start | bytes 6152 | tf_op jit(solution)/shard_map/while/body/eval_jaxpr/ppermute | solution.py:16
  234.2 6.1 %collective-permute-start = (f32[512]{0:T(512)S(1)}, f32[512]{0:T(512)S(1)}, u32[]{:S(2)}, u32[]{:S(2)}) collective-permute-start(f32[512]{0:T(512)S(1)} %add.85), channel_id=1, source_target_pairs={{0,2},{2,4},{4,6},{6,8},{8,10},{10,12},{12,14},{14,16},{16,18},{18... | collective-permute-start | bytes 6152 | tf_op jit(solution)/shard_map/while/body/eval_jaxpr/ppermute | solution.py:16
  245.2 6.1 %collective-permute-start = (f32[512]{0:T(512)S(1)}, f32[512]{0:T(512)S(1)}, u32[]{:S(2)}, u32[]{:S(2)}) collective-permute-start(f32[512]{0:T(512)S(1)} %add.85), channel_id=1, source_target_pairs={{0,2},{2,4},{4,6},{6,8},{8,10},{10,12},{12,14},{14,16},{16,18},{18... | collective-permute-start | bytes 6152 | tf_op jit(solution)/shard_map/while/body/eval_jaxpr/ppermute | solution.py:16
  256.2 6.1 %collective-permute-start = (f32[512]{0:T(512)S(1)}, f32[512]{0:T(512)S(1)}, u32[]{:S(2)}, u32[]{:S(2)}) collective-permute-start(f32[512]{0:T(512)S(1)} %add.85), channel_id=1, source_target_pairs={{0,2},{2,4},{4,6},{6,8},{8,10},{10,12},{12,14},{14,16},{16,18},{18... | collective-permute-start | bytes 6152 | tf_op jit(solution)/shard_map/while/body/eval_jaxpr/ppermute | solution.py:16
  267.2 6.1 %collective-permute-start = (f32[512]{0:T(512)S(1)}, f32[512]{0:T(512)S(1)}, u32[]{:S(2)}, u32[]{:S(2)}) collective-permute-start(f32[512]{0:T(512)S(1)} %add.85), channel_id=1, source_target_pairs={{0,2},{2,4},{4,6},{6,8},{8,10},{10,12},{12,14},{14,16},{16,18},{18... | collective-permute-start | bytes 6152 | tf_op jit(solution)/shard_map/while/body/eval_jaxpr/ppermute | solution.py:16
  278.2 6.1 %collective-permute-start = (f32[512]{0:T(512)S(1)}, f32[512]{0:T(512)S(1)}, u32[]{:S(2)}, u32[]{:S(2)}) collective-permute-start(f32[512]{0:T(512)S(1)} %add.85), channel_id=1, source_target_pairs={{0,2},{2,4},{4,6},{6,8},{8,10},{10,12},{12,14},{14,16},{16,18},{18... | collective-permute-start | bytes 6152 | tf_op jit(solution)/shard_map/while/body/eval_jaxpr/ppermute | solution.py:16
  289.1 6.1 %collective-permute-start = (f32[512]{0:T(512)S(1)}, f32[512]{0:T(512)S(1)}, u32[]{:S(2)}, u32[]{:S(2)}) collective-permute-start(f32[512]{0:T(512)S(1)} %add.85), channel_id=1, source_target_pairs={{0,2},{2,4},{4,6},{6,8},{8,10},{10,12},{12,14},{14,16},{16,18},{18... | collective-permute-start | bytes 6152 | tf_op jit(solution)/shard_map/while/body/eval_jaxpr/ppermute | solution.py:16
  300.1 6.1 %collective-permute-start = (f32[512]{0:T(512)S(1)}, f32[512]{0:T(512)S(1)}, u32[]{:S(2)}, u32[]{:S(2)}) collective-permute-start(f32[512]{0:T(512)S(1)} %add.85), channel_id=1, source_target_pairs={{0,2},{2,4},{4,6},{6,8},{8,10},{10,12},{12,14},{14,16},{16,18},{18... | collective-permute-start | bytes 6152 | tf_op jit(solution)/shard_map/while/body/eval_jaxpr/ppermute | solution.py:16
  311.1 6.1 %collective-permute-start = (f32[512]{0:T(512)S(1)}, f32[512]{0:T(512)S(1)}, u32[]{:S(2)}, u32[]{:S(2)}) collective-permute-start(f32[512]{0:T(512)S(1)} %add.85), channel_id=1, source_target_pairs={{0,2},{2,4},{4,6},{6,8},{8,10},{10,12},{12,14},{14,16},{16,18},{18... | collective-permute-start | bytes 6152 | tf_op jit(solution)/shard_map/while/body/eval_jaxpr/ppermute | solution.py:16
  322.1 6.1 %collective-permute-start = (f32[512]{0:T(512)S(1)}, f32[512]{0:T(512)S(1)}, u32[]{:S(2)}, u32[]{:S(2)}) collective-permute-start(f32[512]{0:T(512)S(1)} %add.85), channel_id=1, source_target_pairs={{0,2},{2,4},{4,6},{6,8},{8,10},{10,12},{12,14},{14,16},{16,18},{18... | collective-permute-start | bytes 6152 | tf_op jit(solution)/shard_map/while/body/eval_jaxpr/ppermute | solution.py:16
  333.1 6.1 %collective-permute-start = (f32[512]{0:T(512)S(1)}, f32[512]{0:T(512)S(1)}, u32[]{:S(2)}, u32[]{:S(2)}) collective-permute-start(f32[512]{0:T(512)S(1)} %add.85), channel_id=1, source_target_pairs={{0,2},{2,4},{4,6},{6,8},{8,10},{10,12},{12,14},{14,16},{16,18},{18... | collective-permute-start | bytes 6152 | tf_op jit(solution)/shard_map/while/body/eval_jaxpr/ppermute | solution.py:16
  339.2 8.4 %copy-start.2 = (f32[512,1024]{1,0:T(8,128)S(1)}, f32[512,1024]{1,0:T(8,128)}, u32[]{:S(2)}) copy-start(f32[512,1024]{1,0:T(8,128)} %copy-done.1) | copy-start | bytes 6291460
Sparse Core Ops, SparseCore 0:
  93.7 14.2 all-gather.8
  123.1 14.8 all-gather.10
where the time goes:
time: 358 us; the launch traced here: 357 us
  blocking collectives  105 us (29%)
  waiting for transfers between devices  77.1 us (22%)
  matrix products  68.2 us (19%)
  local copies, waits for them, and re-layouts  40.7 us (11%)
  starting transfers between devices  35.6 us (10%)
  other arithmetic  16.2 us (5%)
  between operations  13.6 us (4%)
    ppermute x15, waiting for transfers between devices, shifted(): lax.ppermute(value, axis, [(source, source + steps) for source in range(f...  62.7 us
    all_to_all x1, blocking collectives, body(): lax.all_to_all(send_rows, 'tm', split_axis=1, concat_axis=1, tiled=True)  53.8 us
    all_gather x15, blocking collectives, advance(): whole_state = lax.all_gather(state_rows, 'row', axis=0, tiled=True)  43.5 us
    ppermute x15, starting transfers between devices, shifted(): lax.ppermute(value, axis, [(source, source + steps) for source in range(f...  29.1 us
    dot_general x15, matrix products, advance(): jnp.dot(composed, whole_state, precision=lax.Precision.HIGHEST)  28 us
    dot_general x2, matrix products, body(): jnp.dot(information[slab_index], evolve, precision=lax.Precision.HIGHEST)  18.4 us
    gather x1, local copies, waits for them, and re-layouts, body(): padded_values[slot_table].reshape(SLAB_DEV, time_devs, capacity)  13.1 us
    dot_general x1, matrix products, left_product(): new_matrix = jnp.dot(left_rows, pieces[0], precision=lax.Precision.HIGHEST)  9.65 us
  transfers between devices with their start and end apart: 18, of which 17 were waited for; matrix products, arithmetic and copies ran while one was open for 9% of the time, Pallas kernels for 0%

commit v1 on v0

v1 whole, which is shorter than its diff:
```python
import functools

import jax
import jax.numpy as jnp
from jax import lax
from jax.experimental import pallas as pl
from jax.experimental.pallas import tpu as pltpu
from jax.sharding import PartitionSpec as P

CAP = 64
LANES = 128
MESH = pl.DeviceIdType.MESH

sigma_gain = 0.3


def sort_kernel(slabs, target_ref, rows_ref, values_ref, sent_ref, sent_values_ref, slot_ref):
    count = target_ref.shape[1]
    block = 256
    before = (
        lax.broadcasted_iota(jnp.int32, (block, block), 0)
        < lax.broadcasted_iota(jnp.int32, (block, block), 1)
    ).astype(jnp.float32).astype(jnp.bfloat16)
    slab_of = lax.broadcasted_iota(jnp.int32, (slabs, block), 0)
    carry = (slab_of[:, :1] * CAP).astype(jnp.float32)
    for start in range(0, count, block):
        named = (target_ref[:, start : start + block] == slab_of).astype(jnp.float32)
        ahead = jnp.dot(named.astype(jnp.bfloat16), before, preferred_element_type=jnp.float32)
        slot = jnp.sum(named * (ahead + carry), axis=0, keepdims=True)
        slot_ref[:, start : start + block] = slot.astype(jnp.int32)
        carry = carry + jnp.sum(named, axis=1, keepdims=True)

    values = jnp.broadcast_to(values_ref[...].astype(jnp.float32), (8, count)).astype(jnp.bfloat16)

    def place(step, _):
        first = pl.multiple_of(step * block, block)
        wanted = lax.broadcasted_iota(jnp.int32, (block, count), 0) + first
        pick = (wanted == slot_ref[...]).astype(jnp.float32).astype(jnp.bfloat16)
        sent_ref[pl.ds(first, block), :] = jnp.dot(
            pick, rows_ref[...], preferred_element_type=jnp.float32
        ).astype(jnp.bfloat16)
        sent_values_ref[:, pl.ds(first, block)] = lax.dot_general(
            values, pick, (((1,), (1,)), ((), ())), preferred_element_type=jnp.float32
        )[:1].astype(jnp.bfloat16)
        return 0

    lax.fori_loop(0, slabs * CAP // block, place, 0)


def sort_rows(obs_rows, obs_values, target, slabs):
    count, cols = obs_rows.shape
    slots = slabs * CAP
    vmem = pl.BlockSpec(memory_space=pltpu.VMEM)
    return pl.pallas_call(
        functools.partial(sort_kernel, slabs),
        out_shape=(
            jax.ShapeDtypeStruct((slots, cols), jnp.bfloat16),
            jax.ShapeDtypeStruct((1, slots), jnp.bfloat16),
        ),
        in_specs=[vmem] * 3,
        out_specs=(vmem, vmem),
        scratch_shapes=[pltpu.VMEM((1, count), jnp.int32)],
        compiler_params=pltpu.CompilerParams(vmem_limit_bytes=48 << 20),
        name="sort_rows",
    )(target, obs_rows, obs_values)


def chain_kernel(
    devices, a_ref, b_ref, start_ref, out_ref, perm, came, went, back, barred, send_sem, recv_sem
):
    t, r = lax.axis_index("tm"), lax.axis_index("row")
    place = 2 * t + r
    after = (t + r, 1 - r)
    ahead = (t + r - 1, 1 - r)
    subs = came.shape[0]
    state = subs * LANES

    barrier = pltpu.get_barrier_semaphore()

    @pl.when(place > 0)
    def _():
        pl.semaphore_signal(barrier, inc=1, device_id=ahead, device_id_type=MESH)

    @pl.when(place < devices - 1)
    def _():
        pl.semaphore_signal(barrier, inc=1, device_id=after, device_id_type=MESH)

    for sub in range(subs):
        perm[:, sub, :] = a_ref[sub * LANES : (sub + 1) * LANES, :]

    at_end = (place == 0) | (place == devices - 1)

    @pl.when(at_end)
    def _():
        pl.semaphore_wait(barrier, 1)

    @pl.when(jnp.logical_not(at_end))
    def _():
        pl.semaphore_wait(barrier, 2)

    onward = pltpu.make_async_remote_copy(
        src_ref=went, dst_ref=came, send_sem=send_sem.at[0], recv_sem=recv_sem.at[0],
        device_id=after, device_id_type=MESH,
    )
    answer = pltpu.make_async_remote_copy(
        src_ref=went, dst_ref=back, send_sem=send_sem.at[1], recv_sem=recv_sem.at[1],
        device_id=ahead, device_id_type=MESH,
    )

    @pl.when(place == 0)
    def _():
        came[...] = start_ref[...]

    @pl.when(place > 0)
    def _():
        onward.wait_recv()

    entering = came[...]
    pieces = [jnp.broadcast_to(entering[k : k + 1, :], (subs, LANES)) for k in range(subs)]
    lane = lax.broadcasted_iota(jnp.int32, (subs, LANES), 1)
    group = 16

    def rows(step, total):
        for inner in range(group):
            g = step * group + inner
            part = perm[g, :, 0:LANES] * pieces[0]
            for k in range(1, subs):
                part = part + perm[g, :, k * LANES : (k + 1) * LANES] * pieces[k]
            total = jnp.where(lane == g, jnp.sum(part, axis=1, keepdims=True), total)
        return total

    leaving = lax.fori_loop(0, LANES // group, rows, jnp.zeros((subs, LANES), jnp.float32))
    leaving = leaving + b_ref[...]
    went[...] = leaving

    @pl.when(place < devices - 1)
    def _():
        onward.start()

    half = subs // 2

    @pl.when(r == 1)
    def _():
        answer.start()
        out_ref[0] = came[half:, :]
        out_ref[1] = went[half:, :]
        answer.wait_send()

    @pl.when(r == 0)
    def _():
        answer.wait_recv()
        out_ref[0] = went[:half, :]
        out_ref[1] = back[:half, :]

    @pl.when(place < devices - 1)
    def _():
        onward.wait_send()


def run_chain(transition, offset, initial, devices):
    width = transition.shape[0]
    subs = width // LANES
    vmem = pl.BlockSpec(memory_space=pltpu.VMEM)
    small = pltpu.VMEM((subs, LANES), jnp.float32)
    states = pl.pallas_call(
        functools.partial(chain_kernel, devices),
        out_shape=jax.ShapeDtypeStruct((2, subs // 2, LANES), jnp.float32),
        in_specs=[vmem] * 3,
        out_specs=vmem,
        scratch_shapes=[
            pltpu.VMEM((LANES, subs, width), jnp.float32),
            small,
            small,
            small,
            small,
            pltpu.SemaphoreType.DMA((2,)),
            pltpu.SemaphoreType.DMA((2,)),
        ],
        compiler_params=pltpu.CompilerParams(
            collective_id=0, has_side_effects=True, vmem_limit_bytes=48 << 20
        ),
        name="chain",
    )(transition, offset.reshape(subs, LANES), initial.reshape(subs, LANES))
    return states.reshape(2, width // 2)


def split(value):
    high = lax.reduce_precision(value, 8, 7)
    low = lax.reduce_precision(value - high, 8, 7)
    return high.astype(jnp.bfloat16), low.astype(jnp.bfloat16)


def dot32(left, right, dims):
    return lax.dot_general(left, right, (dims, ((), ())), preferred_element_type=jnp.float32)


def body(initial, dynamics, obs_rows, obs_values, obs_slab):
    time_devs = lax.axis_size("tm")
    row_devs = lax.axis_size("row")
    width = dynamics.shape[1]
    cols = obs_rows.shape[1]
    slabs = time_devs * row_devs
    sent, sent_values = sort_rows(
        obs_rows, obs_values.reshape(1, -1), obs_slab.reshape(1, -1), slabs
    )
    axes = ("tm", "row")
    got = lax.all_to_all(
        sent.reshape(slabs, CAP, cols), axes, split_axis=0, concat_axis=0, tiled=True
    )
    got_values = lax.all_to_all(
        sent_values.reshape(slabs, CAP), axes, split_axis=0, concat_axis=0, tiled=True
    )
    got = got.reshape(time_devs, row_devs, CAP, cols)
    values = got_values.reshape(time_devs, row_devs, CAP)[:, 0].reshape(1, -1)
    rows = got.transpose(0, 2, 1, 3).reshape(time_devs * CAP, width)
    high, low = split(dynamics)
    seen = rows.astype(jnp.float32) + (
        dot32(rows, high, ((1,), (0,))) + dot32(rows, low, ((1,), (0,)))
    )
    seen_high, seen_low = split(seen)
    gain = dot32(rows, seen_high, ((0,), (0,))) + dot32(rows, seen_low, ((0,), (0,)))
    transition = jnp.eye(width, dtype=jnp.float32) + dynamics - sigma_gain * gain
    offset = sigma_gain * dot32(values, rows, ((1,), (0,)))
    return run_chain(transition, offset, initial, slabs)


def solution(mesh):
    placed = (P(), P(), P("tm", "row"), P("tm"), P("tm", None))
    return jax.shard_map(
        body, mesh=mesh, in_specs=placed, out_specs=P("tm", "row"), check_vma=False
    )
```

time: 358 us -> 172 us (0.48)
  the two profiles are of different devices: /device:TPU:9 before, /device:TPU:31 now
where the time goes in v1:
time: 172 us
  Pallas kernels  90.9 us (53%)
  waiting for transfers between devices  46.8 us (27%)
  matrix products  10.4 us (6%)
  starting transfers between devices  7.92 us (5%)
  blocking collectives  7.9 us (5%)
  local copies, waits for them, and re-layouts  7.74 us (4%)
    pallas_call x1, Pallas kernels, run_chain(): pl.pallas_call(functools.partial(chain_kernel, devices), out_shape=jax.Sh...  81.9 us
    all_to_all x1, waiting for transfers between devices, body(): lax.all_to_all(sent.reshape(slabs, CAP, cols), axes, split_axis=0, concat...  46.8 us
    dot_general x5, matrix products, dot32(): lax.dot_general(left, right, (dims, ((), ())), preferred_element_type=jnp...  10.4 us
    pallas_call x1, Pallas kernels, sort_rows(): pl.pallas_call(functools.partial(sort_kernel, slabs), out_shape=(jax.Shap...  9.05 us
    all_to_all x1, starting transfers between devices, body(): lax.all_to_all(sent.reshape(slabs, CAP, cols), axes, split_axis=0, concat...  7.92 us
    all_to_all x1, blocking collectives, body(): lax.all_to_all(sent_values.reshape(slabs, CAP), axes, split_axis=0, conca...  7.9 us
    unnamed x11, local copies, waits for them, and re-layouts  4.68 us
  transfers between devices with their start and end apart: 1, of which 1 were waited for; matrix products, arithmetic and copies ran while one was open for 0% of the time, Pallas kernels for 0%

profile of v1, /device:TPU:31, one launch (start us, length us, event | category | flops | bytes accessed | tf_op | source)
XLA Modules:
  0.0 171.8 jit_solution(5878682292111432347)
XLA Ops:
  0.0 0.7 reshape.40.values_ref
  0.7 0.0 copy-start
  0.7 1.6 copy-done
  2.3 0.0 copy-start.1
  2.3 0.7 copy-done.1
  3.0 9.1 %sort_rows.1 = (bf16[2048,512]{1,0:T(8,128)(2,1)}, bf16[1,2048]{1,0:T(2,128)(2,1)S(1)}) custom-call(s32[1,2048]{1,0:T(1,128)S(1)} %bitcast.23, bf16[2048,512]{1,0:T(8,128)(2,1)S(1)} %copy-done, bf16[1,2048]{1,0:T(2,128)(2,1)S(1)} %reshape.40.values_ref), custom_call_target="tpu_custom_call" | custom-call | tf_op jit(solution)/shard_map/sort_rows/pallas_call | solution.py:54
  12.1 0.1 all_to_all.12
  12.2 7.9 %all_to_all.15 = bf16[32,1,64]{2,1,0:T(2,128)(2,1)S(1)} all-to-all(bf16[32,1,64]{2,1,0:T(2,128)(2,1)S(1)} %all_to_all.12), channel_id=1, replica_groups=mesh['tm'=16,'row'=2] {'tm','row'}, dimensions={0} | all-to-all | bytes 8192 | tf_op jit(solution)/shard_map/all_to_all | solution.py:210
  20.1 7.9 %all-to-all-start = ((bf16[32,64,512]{2,1,0:T(8,128)(2,1)}), bf16[32,64,512]{2,1,0:T(8,128)(2,1)S(1)}, u32[]{:S(2)}, u32[]{:S(2)}) async-start(bf16[32,64,512]{2,1,0:T(8,128)(2,1)} %bitcast.1), calls=%async_computation | async-start | bytes 4194304 | tf_op jit(solution)/shard_map/all_to_all | solution.py:207
  28.0 0.1 reshape.49
  28.1 46.8 %all-to-all-done = bf16[32,64,512]{2,1,0:T(8,128)(2,1)S(1)} async-done(((bf16[32,64,512]{2,1,0:T(8,128)(2,1)}), bf16[32,64,512]{2,1,0:T(8,128)(2,1)S(1)}, u32[]{:S(2)}, u32[]{:S(2)}) %all-to-all-start) | async-done | bytes 2097184 | tf_op jit(solution)/shard_map/all_to_all | solution.py:207
  74.9 2.2 %copy.9 = bf16[16,2,64,512]{3,1,2,0:T(2,128)(2,1)S(1)} copy(bf16[16,2,64,512]{3,2,1,0:T(8,128)(2,1)S(1)} %bitcast.25) | data formatting | bytes 4194304 | tf_op jit(solution)/shard_map/reshape | solution.py:213
  77.0 0.0 copy-start.3
  77.0 0.6 copy.12
  77.6 0.4 fusion.10
  78.0 1.2 copy-done.3
  79.2 2.4 %fusion.6 = f32[1024,1024]{1,0:T(8,128)S(1)} fusion(bf16[1024,1024]{1,0:T(8,128)(2,1)S(1)} %bitcast.27, f32[1024,1024]{1,0:T(8,128)S(1)} %copy-done.3), kind=kOutput, calls=%fused_computation.12 | convolution fusion | flops 2151677952 | bytes 10485760 | tf_op jit(solution)/shard_map/dot_general | solution.py:194
  81.6 2.4 %add_add_fusion = f32[1024,1024]{1,0:T(8,128)S(1)} fusion(f32[1024,1024]{1,0:T(8,128)S(1)} %fusion.6, bf16[1024,1024]{1,0:T(8,128)(2,1)S(1)} %bitcast.28, f32[1024,1024]{1,0:T(8,128)S(1)} %copy-done.3), kind=kOutput, calls=%fused_computation.9 | convolution fusion | flops 2152726528 | bytes 14680064 | tf_op jit(solution)/shard_map/dot_general | solution.py:194
  84.0 2.4 %fusion.4 = f32[1024,1024]{1,0:T(8,128)S(1)} fusion(bf16[1024,1024]{1,0:T(8,128)(2,1)S(1)} %bitcast.29, f32[1024,1024]{1,0:T(8,128)S(1)} %add_add_fusion), kind=kOutput, calls=%fused_computation.11 | convolution fusion | flops 2151677952 | bytes 10485760 | tf_op jit(solution)/shard_map/dot_general | solution.py:194
  86.4 0.0 copy-start.2
  86.5 2.8 %multiply_subtract_fusion.a_ref = f32[1024,1024]{1,0:T(8,128)S(1)} fusion(f32[1024,1024]{1,0:T(8,128)S(1)} %fusion.4, f32[1024,1024]{1,0:T(8,128)S(1)} %copy-done.3, bf16[1024,1024]{1,0:T(8,128)(2,1)S(1)} %bitcast.30, f32[1024,1024]{1,0:T(8,128)S(1)} %add_add_fusion), kind=kOutput, calls=%fused_computation.8 | convolution fusion | flops 2155872256 | bytes 18874368 | tf_op jit(solution)/shard_map/dot_general | solution.py:194
  89.3 0.0 copy-done.2
  89.3 81.9 %chain.1 = f32[2,4,128]{2,1,0:T(4,128)S(1)} custom-call(f32[1024,1024]{1,0:T(8,128)S(1)} %multiply_subtract_fusion.a_ref, f32[8,128]{1,0:T(8,128)S(1)} %multiply_bitcast_fusion.b_ref, f32[8,128]{1,0:T(8,128)S(1)} %bitcast.24), custom_call_target="tpu_custom_call" | custom-call | tf_op jit(solution)/shard_map/chain/pallas_call | solution.py:165
  171.2 0.6 copy.15
  (4 shorter events, 0.1 us)
Async XLA Ops:
  0.7 1.6 copy-start
  2.3 0.7 copy-start.1
  20.1 54.8 %all-to-all-start = ((bf16[32,64,512]{2,1,0:T(8,128)(2,1)}), bf16[32,64,512]{2,1,0:T(8,128)(2,1)S(1)}, u32[]{:S(2)}, u32[]{:S(2)}) async-start(bf16[32,64,512]{2,1,0:T(8,128)(2,1)} %bitcast.1), calls=%async_computation | async-start | bytes 4194304 | tf_op jit(solution)/shard_map/all_to_all | solution.py:207
  77.0 2.2 %copy-start.3 = (f32[1024,1024]{1,0:T(8,128)S(1)}, f32[1024,1024]{1,0:T(8,128)}, u32[]{:S(2)}) copy-start(f32[1024,1024]{1,0:T(8,128)} %param.6) | copy-start | bytes 12582916
  86.4 2.9 %copy-start.2 = (f32[1024]{0:T(1024)S(1)}, f32[1024]{0:T(1024)}, u32[]{:S(2)}) copy-start(f32[1024]{0:T(1024)} %param.5) | copy-start | bytes 12292

commit v2 on v1

v2 whole, which is shorter than its diff:
```python
import jax
import jax.numpy as jnp
from jax import lax
from jax.experimental import pallas as pl
from jax.experimental.pallas import tpu as pltpu
from jax.sharding import PartitionSpec as P

CAP = 64
LANES = 128
MESH = pl.DeviceIdType.MESH

sigma_gain = 0.3


def route_kernel(
    target_ref, rows_ref, values_ref, got_ref, got_values_ref,
    sent, sent_values, slot_ref, row_send, row_recv, value_send, value_recv, own_sem,
):
    time_devs, row_devs = lax.axis_size("tm"), lax.axis_size("row")
    slabs = time_devs * row_devs
    me = lax.axis_index("tm") * row_devs + lax.axis_index("row")
    count = target_ref.shape[1]
    block = 256
    share = block // CAP
    blocks = slabs // share

    def device(slab):
        return (slab // row_devs, lax.rem(slab, row_devs))

    barrier = pltpu.get_barrier_semaphore()

    def greet(slab, _):
        @pl.when(slab != me)
        def _():
            pl.semaphore_signal(barrier, inc=1, device_id=device(slab), device_id_type=MESH)

        return 0

    lax.fori_loop(0, slabs, greet, 0)

    before = (
        lax.broadcasted_iota(jnp.int32, (block, block), 0)
        < lax.broadcasted_iota(jnp.int32, (block, block), 1)
    ).astype(jnp.float32).astype(jnp.bfloat16)
    slab_of = lax.broadcasted_iota(jnp.int32, (slabs, block), 0)
    carry = (slab_of[:, :1] * CAP).astype(jnp.float32)
    for start in range(0, count, block):
        named = (target_ref[:, start : start + block] == slab_of).astype(jnp.float32)
        ahead = jnp.dot(named.astype(jnp.bfloat16), before, preferred_element_type=jnp.float32)
        slot = jnp.sum(named * (ahead + carry), axis=0, keepdims=True)
        slot_ref[:, start : start + block] = slot.astype(jnp.int32)
        carry = carry + jnp.sum(named, axis=1, keepdims=True)

    values = jnp.broadcast_to(values_ref[...].astype(jnp.float32), (8, count)).astype(jnp.bfloat16)
    sent_values[...] = jnp.zeros_like(sent_values)

    def copies(slab, source):
        rows = pltpu.make_async_remote_copy(
            src_ref=sent.at[slab], dst_ref=got_ref.at[source],
            send_sem=row_send.at[slab], recv_sem=row_recv.at[source],
            device_id=device(slab), device_id_type=MESH,
        )
        tags = pltpu.make_async_remote_copy(
            src_ref=sent_values.at[slab], dst_ref=got_values_ref.at[source],
            send_sem=value_send.at[slab], recv_sem=value_recv.at[source],
            device_id=device(slab), device_id_type=MESH,
        )
        return rows, tags

    keep = (
        pltpu.make_async_copy(sent.at[me], got_ref.at[me], own_sem.at[0]),
        pltpu.make_async_copy(sent_values.at[me], got_values_ref.at[me], own_sem.at[1]),
    )

    def place(at):
        first = at * share
        wanted = lax.broadcasted_iota(jnp.int32, (block, count), 0) + first * CAP
        pick = (wanted == slot_ref[...]).astype(jnp.float32).astype(jnp.bfloat16)
        rows = jnp.dot(pick, rows_ref[...], preferred_element_type=jnp.float32).astype(jnp.bfloat16)
        tags = lax.dot_general(
            values, pick, (((1,), (1,)), ((), ())), preferred_element_type=jnp.float32
        )[:1]
        for inner in range(share):
            sent[first + inner] = rows[inner * CAP : (inner + 1) * CAP]
            sent_values[first + inner, :, :CAP] = tags[:, inner * CAP : (inner + 1) * CAP]

    def send(at):
        for inner in range(share):
            slab = at * share + inner

            @pl.when(slab != me)
            def _():
                for copy in copies(slab, me):
                    copy.start()

            @pl.when(slab == me)
            def _():
                for copy in keep:
                    copy.start()

    mine = me // share
    place(mine)
    pl.semaphore_wait(barrier, slabs - 1)
    send(mine)

    def step(turn, _):
        at = lax.rem(mine + turn, blocks)
        place(at)
        send(at)
        return 0

    lax.fori_loop(1, blocks, step, 0)

    def finish(slab, _):
        @pl.when(slab != me)
        def _():
            for copy in copies(slab, slab):
                copy.wait_recv()
                copy.wait_send()

        return 0

    lax.fori_loop(0, slabs, finish, 0)
    for copy in keep:
        copy.wait()


def route(obs_rows, obs_values, target, slabs):
    count, cols = obs_rows.shape
    vmem = pl.BlockSpec(memory_space=pltpu.VMEM)
    sems = pltpu.SemaphoreType.DMA((slabs,))
    return pl.pallas_call(
        route_kernel,
        out_shape=(
            jax.ShapeDtypeStruct((slabs, CAP, cols), jnp.bfloat16),
            jax.ShapeDtypeStruct((slabs, 1, LANES), jnp.float32),
        ),
        in_specs=[vmem] * 3,
        out_specs=(vmem, vmem),
        scratch_shapes=[
            pltpu.VMEM((slabs, CAP, cols), jnp.bfloat16),
            pltpu.VMEM((slabs, 1, LANES), jnp.float32),
            pltpu.VMEM((1, count), jnp.int32),
            sems,
            sems,
            sems,
            sems,
            pltpu.SemaphoreType.DMA((2,)),
        ],
        compiler_params=pltpu.CompilerParams(
            collective_id=1, has_side_effects=True, vmem_limit_bytes=56 << 20
        ),
        name="route",
    )(target, obs_rows, obs_values)


def chain_kernel(
    high_ref, low_ref, b_ref, start_ref, out_ref,
    perm, high_got, low_got, b_got, came, went, back, offset, send_sem, recv_sem, tile_send, tile_recv,
):
    t, r = lax.axis_index("tm"), lax.axis_index("row")
    last = lax.axis_size("tm") - 1
    partner = (t, 1 - r)
    subs = came.shape[0]
    width = subs * LANES
    tile = 256
    tiles = width // tile

    barrier = pltpu.get_barrier_semaphore()

    def greet(peer):
        pl.semaphore_signal(barrier, inc=1, device_id=peer, device_id_type=MESH)

    greet(partner)

    @pl.when(t > 0)
    def _():
        greet((t - 1, 1))

    @pl.when((r == 1) & (t < last))
    def _():
        greet((t + 1, 0))
        greet((t + 1, 1))

    peers = 1 + jnp.where(t > 0, 1, 0) + jnp.where((r == 1) & (t < last), 2, 0)
    pl.semaphore_wait(barrier, peers)

    def push(source, target, index, peer):
        return pltpu.make_async_remote_copy(
            src_ref=source, dst_ref=target, send_sem=send_sem.at[index],
            recv_sem=recv_sem.at[index], device_id=peer, device_id_type=MESH,
        )

    lend = push(b_ref, b_got, 0, partner)
    answer = push(went, back, 1, partner)
    onward = push(went, came, 2, (t + 1, 1))
    aside = pltpu.make_async_remote_copy(
        src_ref=went, dst_ref=came, send_sem=send_sem.at[3],
        recv_sem=recv_sem.at[2], device_id=(t + 1, 0), device_id_type=MESH,
    )

    def part(k):
        cols = pl.ds(pl.multiple_of(k * tile, tile), tile)
        return [
            pltpu.make_async_remote_copy(
                src_ref=source.at[:, cols], dst_ref=target.at[:, cols],
                send_sem=tile_send.at[index, k], recv_sem=tile_recv.at[index, k],
                device_id=partner, device_id_type=MESH,
            )
            for index, (source, target) in enumerate(((high_ref, high_got), (low_ref, low_got)))
        ]

    @pl.when(r == 0)
    def _():
        lend.start()
        for k in range(tiles):
            for copy in part(k):
                copy.start()

    for sub in range(subs):
        own = slice(sub * LANES, (sub + 1) * LANES)
        perm[:, sub, :] = high_ref[own, :].astype(jnp.float32) + low_ref[own, :].astype(jnp.float32)

    lane = lax.broadcasted_iota(jnp.int32, (subs, LANES), 1)
    group = 16

    def apply(vector):
        pieces = [jnp.broadcast_to(vector[k : k + 1, :], (subs, LANES)) for k in range(subs)]

        def rows(step, total):
            for inner in range(group):
                g = step * group + inner
                part = perm[g, :, 0:LANES] * pieces[0]
                for k in range(1, subs):
                    part = part + perm[g, :, k * LANES : (k + 1) * LANES] * pieces[k]
                total = jnp.where(lane == g, jnp.sum(part, axis=1, keepdims=True), total)
            return total

        return lax.fori_loop(0, LANES // group, rows, jnp.zeros((subs, LANES), jnp.float32))

    offset[...] = b_ref[...]

    @pl.when(r == 1)
    def _():
        lend.wait_recv()
        offset[...] = apply(b_got[...]) + b_ref[...]

        def compose(k, _):
            for copy in part(k):
                copy.wait_recv()
            cols = pl.ds(pl.multiple_of(k * tile, tile), tile)
            high, low = high_got[:, cols], low_got[:, cols]
            whole = (
                jnp.dot(high_ref[...], high, preferred_element_type=jnp.float32)
                + jnp.dot(high_ref[...], low, preferred_element_type=jnp.float32)
                + jnp.dot(low_ref[...], high, preferred_element_type=jnp.float32)
            )
            for sub in range(subs):
                perm[:, sub, cols] = whole[sub * LANES : (sub + 1) * LANES, :]
            return 0

        lax.fori_loop(0, tiles, compose, 0)

    @pl.when(r == 0)
    def _():
        lend.wait_send()

        def drain(k, _):
            for copy in part(k):
                copy.wait_send()
            return 0

        lax.fori_loop(0, tiles, drain, 0)

    @pl.when(t == 0)
    def _():
        came[...] = start_ref[...]

    @pl.when(t > 0)
    def _():
        onward.wait_recv()

    went[...] = apply(came[...]) + offset[...]
    passing = (r == 1) & (t < last)

    @pl.when(passing)
    def _():
        onward.start()
        aside.start()

    answer.start()
    answer.wait()
    half = subs // 2

    @pl.when(r == 0)
    def _():
        out_ref[0] = went[:half, :]
        out_ref[1] = back[:half, :]

    @pl.when(r == 1)
    def _():
        out_ref[0] = back[half:, :]
        out_ref[1] = went[half:, :]

    @pl.when(passing)
    def _():
        onward.wait_send()
        aside.wait_send()


def run_chain(high, low, offset, initial):
    width = high.shape[0]
    subs = width // LANES
    tiles = width // 256
    vmem = pl.BlockSpec(memory_space=pltpu.VMEM)
    small = pltpu.VMEM((subs, LANES), jnp.float32)
    states = pl.pallas_call(
        chain_kernel,
        out_shape=jax.ShapeDtypeStruct((2, subs // 2, LANES), jnp.float32),
        in_specs=[vmem] * 4,
        out_specs=vmem,
        scratch_shapes=[
            pltpu.VMEM((LANES, subs, width), jnp.float32),
            pltpu.VMEM((width, width), jnp.bfloat16),
            pltpu.VMEM((width, width), jnp.bfloat16),
            small,
            small,
            small,
            small,
            small,
            pltpu.SemaphoreType.DMA((4,)),
            pltpu.SemaphoreType.DMA((3,)),
            pltpu.SemaphoreType.DMA((2, tiles)),
            pltpu.SemaphoreType.DMA((2, tiles)),
        ],
        compiler_params=pltpu.CompilerParams(
            collective_id=0, has_side_effects=True, vmem_limit_bytes=48 << 20
        ),
        name="chain",
    )(high, low, offset.reshape(subs, LANES), initial.reshape(subs, LANES))
    return states.reshape(2, width // 2)


def split(value):
    high = lax.reduce_precision(value, 8, 7)
    low = lax.reduce_precision(value - high, 8, 7)
    return high.astype(jnp.bfloat16), low.astype(jnp.bfloat16)


def dot32(left, right, dims):
    return lax.dot_general(left, right, (dims, ((), ())), preferred_element_type=jnp.float32)


def body(initial, dynamics, obs_rows, obs_values, obs_slab):
    time_devs = lax.axis_size("tm")
    row_devs = lax.axis_size("row")
    width = dynamics.shape[1]
    cols = obs_rows.shape[1]
    slabs = time_devs * row_devs
    got, got_values = route(obs_rows, obs_values.reshape(1, -1), obs_slab.reshape(1, -1), slabs)
    got = got.reshape(time_devs, row_devs, CAP, cols)
    values = got_values[:, 0, :CAP].astype(jnp.bfloat16).reshape(time_devs, row_devs, CAP)[:, 0].reshape(1, -1)
    rows = got.transpose(0, 2, 1, 3).reshape(time_devs * CAP, width)
    high, low = split(dynamics)
    seen = rows.astype(jnp.float32) + (
        dot32(rows, high, ((1,), (0,))) + dot32(rows, low, ((1,), (0,)))
    )
    seen_high, seen_low = split(seen)
    gain = dot32(rows, seen_high, ((0,), (0,))) + dot32(rows, seen_low, ((0,), (0,)))
    transition = jnp.eye(width, dtype=jnp.float32) + dynamics - sigma_gain * gain
    offset = sigma_gain * dot32(values, rows, ((1,), (0,)))
    return run_chain(*split(transition), offset, initial)


def solution(mesh):
    placed = (P(), P(), P("tm", "row"), P("tm"), P("tm", None))
    return jax.shard_map(
        body, mesh=mesh, in_specs=placed, out_specs=P("tm", "row"), check_vma=False
    )
```

time: 172 us -> 128 us (0.74)
  waiting for transfers between devices: 46.8 us -> 0 us
  Pallas kernels: 90.9 us -> 108 us
  starting transfers between devices: 7.92 us -> 0 us
  blocking collectives: 7.9 us -> 0 us
  matrix products: 10.4 us -> 13.5 us
    all_to_all x1 -> x0, waiting for transfers between devices: 46.8 us -> none  [body(): lax.all_to_all(sent.reshape(slabs, CAP, cols), axes, split_axis=0, concat...]
    pallas_call x2, Pallas kernels: 90.9 us -> 108 us  [the longest x1 60.2 us: route(): pl.pallas_call(route_kernel, out_shape=(jax.ShapeDtypeStruct((slabs, CAP,...]
    all_to_all x1 -> x0, starting transfers between devices: 7.92 us -> none  [body(): lax.all_to_all(sent.reshape(slabs, CAP, cols), axes, split_axis=0, concat...]
    all_to_all x1 -> x0, blocking collectives: 7.9 us -> none  [body(): lax.all_to_all(sent_values.reshape(slabs, CAP), axes, split_axis=0, conca...]
    transpose x0 -> x1, local copies, waits for them, and re-layouts: none -> 3.76 us  [body(): rows = got.transpose(0, 2, 1, 3).reshape(time_devs * CAP, width)]
    unnamed x11 -> x9, local copies, waits for them, and re-layouts: 4.68 us -> 1.18 us
    dot_general x5, matrix products: 10.4 us -> 13.5 us  [dot32(): lax.dot_general(left, right, (dims, ((), ())), preferred_element_type=jnp...]
    reshape x2 -> x1, local copies, waits for them, and re-layouts: 2.25 us -> 0.09 us  [the longest x1 2.16 us: body(): got = got.reshape(time_devs, row_devs, CAP, cols)]
  transfers between devices with their start and end apart: 1 -> 0, of which waited for: 1 -> 0; matrix products, arithmetic and copies ran while one was open for 0% -> 0% of each run, Pallas kernels for 0% -> 0%
where the time goes in v2:
time: 128 us
  Pallas kernels  108 us (84%)
  matrix products  13.5 us (11%)
  local copies, waits for them, and re-layouts  6.36 us (5%)
    pallas_call x1, Pallas kernels, route(): pl.pallas_call(route_kernel, out_shape=(jax.ShapeDtypeStruct((slabs, CAP,...  60.2 us
    pallas_call x1, Pallas kernels, run_chain(): pl.pallas_call(chain_kernel, out_shape=jax.ShapeDtypeStruct((2, subs // 2...  48 us
    dot_general x5, matrix products, dot32(): lax.dot_general(left, right, (dims, ((), ())), preferred_element_type=jnp...  13.5 us
    transpose x1, local copies, waits for them, and re-layouts, body(): rows = got.transpose(0, 2, 1, 3).reshape(time_devs * CAP, width)  3.76 us

profile of v2, /device:TPU:31, one launch (start us, length us, event | category | flops | bytes accessed | tf_op | source)
XLA Modules:
  0.0 128.1 jit_solution(6382254910161283249)
XLA Ops:
  0.0 1.3 %reshape.32.values_ref = bf16[1,2048]{1,0:T(2,128)(2,1)} reshape(bf16[2048]{0:T(1024)(128)(2,1)} %param.8) | data formatting | bytes 8192 | tf_op jit(solution)/shard_map/reshape | solution.py:360
  1.3 60.2 %route.1 = (bf16[32,64,512]{2,1,0:T(8,128)(2,1)}, f32[32,1,128]{2,1,0:T(1,128)}) custom-call(s32[1,2048]{1,0:T(1,128)} %bitcast.33, bf16[2048,512]{1,0:T(8,128)(2,1)} %rows_ref.1, bf16[1,2048]{1,0:T(2,128)(2,1)} %reshape.32.values_ref), custom_call_target="tpu_custom_call" | custom-call | tf_op jit(solution)/shard_map/route/pallas_call | solution.py:132
  61.5 0.0 copy-start.1
  61.5 3.8 %copy.7 = bf16[16,64,2,512]{3,2,1,0:T(2,128)(2,1)S(1)} copy(bf16[16,64,2,512]{3,1,2,0:T(8,128)(2,1)} %bitcast.30) | data formatting | bytes 4194304 | tf_op jit(solution)/shard_map/transpose | solution.py:363
  65.2 0.6 copy.9
  65.8 0.0 copy-done.1
  65.9 0.1 reshape.39
  66.0 0.4 fusion.12
  66.4 0.0 copy-start.2
  66.4 4.7 %fusion.8 = f32[1024,1024]{1,0:T(8,128)S(1)} fusion(bf16[1024,1024]{1,0:T(8,128)(2,1)S(1)} %bitcast.25, f32[1024,1024]{1,0:T(8,128)} %param.6), kind=kOutput, calls=%fused_computation.16 | convolution fusion | flops 2151677952 | bytes 10485760 | tf_op jit(solution)/shard_map/dot_general | solution.py:351
  71.0 0.0 copy-done.2
  71.1 2.4 %add_add_fusion = f32[1024,1024]{1,0:T(8,128)S(1)} fusion(f32[1024,1024]{1,0:T(8,128)S(1)} %fusion.8, bf16[1024,1024]{1,0:T(8,128)(2,1)S(1)} %bitcast.26, f32[1024,1024]{1,0:T(8,128)S(1)} %copy-done.2), kind=kOutput, calls=%fused_computation.13 | convolution fusion | flops 2152726528 | bytes 14680064 | tf_op jit(solution)/shard_map/dot_general | solution.py:351
  73.5 2.5 %fusion.6 = f32[1024,1024]{1,0:T(8,128)S(1)} fusion(bf16[1024,1024]{1,0:T(8,128)(2,1)S(1)} %bitcast.27, f32[1024,1024]{1,0:T(8,128)S(1)} %add_add_fusion), kind=kOutput, calls=%fused_computation.15 | convolution fusion | flops 2151677952 | bytes 10485760 | tf_op jit(solution)/shard_map/dot_general | solution.py:351
  76.0 0.0 copy-start
  76.0 3.5 %fusion.5 = (bf16[1024,1024]{1,0:T(8,128)(2,1)S(1)}, bf16[1024,1024]{1,0:T(8,128)(2,1)S(1)}) fusion(f32[1024,1024]{1,0:T(8,128)S(1)} %fusion.6, bf16[1024,1024]{1,0:T(8,128)(2,1)S(1)} %bitcast.28, f32[1024,1024]{1,0:T(8,128)S(1)} %add_add_fusion, f32[1024,1024]{1,0:T(8,128)S(1)} %copy-done.2), kind=kOutput, calls=%fused_computation.11 | convolution fusion | flops 2161115136 | bytes 18874368 | tf_op jit(solution)/shard_map/dot_general | solution.py:351
  79.5 0.0 copy-done
  79.5 48.0 %chain.1 = f32[2,4,128]{2,1,0:T(4,128)S(1)} custom-call(bf16[1024,1024]{1,0:T(8,128)(2,1)S(1)} %get-tuple-element.10.high_ref, bf16[1024,1024]{1,0:T(8,128)(2,1)S(1)} %get-tuple-element.9.low_ref, f32[8,128]{1,0:T(8,128)S(1)} %multiply_bitcast_fusion.b_ref, f32[8,128]{1,0:T(8,128)S(1)} %bitcast.23), custom_call_target="tpu_custom_call" | custom-call | tf_op jit(solution)/shard_map/chain/pallas_call | solution.py:317
  127.6 0.6 copy.12
  (4 shorter events, 0.1 us)
Async XLA Ops:
  61.5 4.3 %copy-start.1 = (f32[32,1,128]{2,1,0:T(1,128)S(1)}, f32[32,1,128]{2,1,0:T(1,128)}, u32[]{:S(2)}) copy-start(f32[32,1,128]{2,1,0:T(1,128)} %get-tuple-element.8) | copy-start | bytes 49156
  66.4 4.7 %copy-start.2 = (f32[1024,1024]{1,0:T(8,128)S(1)}, f32[1024,1024]{1,0:T(8,128)}, u32[]{:S(2)}) copy-start(f32[1024,1024]{1,0:T(8,128)} %param.6) | copy-start | bytes 12582916
  76.0 3.5 %copy-start = (f32[1024]{0:T(1024)S(1)}, f32[1024]{0:T(1024)}, u32[]{:S(2)}) copy-start(f32[1024]{0:T(1024)} %param.5) | copy-start | bytes 12292

commit v3 on v2

--- a/solution.py
+++ b/solution.py
@@ -12,14 +12,23 @@
 sigma_gain = 0.3
 
 
-def route_kernel(
-    target_ref, rows_ref, values_ref, got_ref, got_values_ref,
-    sent, sent_values, slot_ref, row_send, row_recv, value_send, value_recv, own_sem,
+def observer_kernel(
+    target_ref, rows_ref, values_ref, dynamics_ref, start_ref, out_ref,
+    sent, sent_values, slot_ref, got, got_values, dynamics, dyn_high, dyn_low, turned, gain, moment,
+    high_ref, low_ref, b_ref, perm, high_got, low_got, b_got, came, went, back, offset,
+    row_send, row_recv, value_send, value_recv, own_sem, send_sem, recv_sem, tile_send, tile_recv,
 ):
     time_devs, row_devs = lax.axis_size("tm"), lax.axis_size("row")
+    t, r = lax.axis_index("tm"), lax.axis_index("row")
     slabs = time_devs * row_devs
-    me = lax.axis_index("tm") * row_devs + lax.axis_index("row")
-    count = target_ref.shape[1]
+    last = time_devs - 1
+    me = t * row_devs + r
+    partner = (t, 1 - r)
+    count, local = rows_ref.shape
+    width = local * row_devs
+    subs = width // LANES
+    tile = 256
+    tiles = width // tile
     block = 256
     share = block // CAP
     blocks = slabs // share
@@ -37,6 +46,8 @@
         return 0
 
     lax.fori_loop(0, slabs, greet, 0)
+    fetch = pltpu.make_async_copy(dynamics_ref, dynamics, own_sem.at[2])
+    fetch.start()
 
     before = (
         lax.broadcasted_iota(jnp.int32, (block, block), 0)
@@ -54,22 +65,27 @@
     values = jnp.broadcast_to(values_ref[...].astype(jnp.float32), (8, count)).astype(jnp.bfloat16)
     sent_values[...] = jnp.zeros_like(sent_values)
 
+    def landing(source):
+        rows = pl.ds(pl.multiple_of(source // row_devs * CAP, CAP), CAP)
+        cols = pl.ds(pl.multiple_of(lax.rem(source, row_devs) * local, local), local)
+        return got.at[rows, cols]
+
     def copies(slab, source):
         rows = pltpu.make_async_remote_copy(
-            src_ref=sent.at[slab], dst_ref=got_ref.at[source],
+            src_ref=sent.at[slab], dst_ref=landing(source),
             send_sem=row_send.at[slab], recv_sem=row_recv.at[source],
             device_id=device(slab), device_id_type=MESH,
         )
         tags = pltpu.make_async_remote_copy(
-            src_ref=sent_values.at[slab], dst_ref=got_values_ref.at[source],
+            src_ref=sent_values.at[slab], dst_ref=got_values.at[source],
             send_sem=value_send.at[slab], recv_sem=value_recv.at[source],
             device_id=device(slab), device_id_type=MESH,
         )
         return rows, tags
 
     keep = (
-        pltpu.make_async_copy(sent.at[me], got_ref.at[me], own_sem.at[0]),
-        pltpu.make_async_copy(sent_values.at[me], got_values_ref.at[me], own_sem.at[1]),
+        pltpu.make_async_copy(sent.at[me], landing(me), own_sem.at[0]),
+        pltpu.make_async_copy(sent_values.at[me], got_values.at[me], own_sem.at[1]),
     )
 
     def place(at):
@@ -111,79 +127,68 @@
 
     lax.fori_loop(1, blocks, step, 0)
 
-    def finish(slab, _):
-        @pl.when(slab != me)
-        def _():
-            for copy in copies(slab, slab):
-                copy.wait_recv()
-                copy.wait_send()
-
-        return 0
-
-    lax.fori_loop(0, slabs, finish, 0)
-    for copy in keep:
-        copy.wait()
-
-
-def route(obs_rows, obs_values, target, slabs):
-    count, cols = obs_rows.shape
-    vmem = pl.BlockSpec(memory_space=pltpu.VMEM)
-    sems = pltpu.SemaphoreType.DMA((slabs,))
-    return pl.pallas_call(
-        route_kernel,
-        out_shape=(
-            jax.ShapeDtypeStruct((slabs, CAP, cols), jnp.bfloat16),
-            jax.ShapeDtypeStruct((slabs, 1, LANES), jnp.float32),
-        ),
-        in_specs=[vmem] * 3,
-        out_specs=(vmem, vmem),
-        scratch_shapes=[
-            pltpu.VMEM((slabs, CAP, cols), jnp.bfloat16),
-            pltpu.VMEM((slabs, 1, LANES), jnp.float32),
-            pltpu.VMEM((1, count), jnp.int32),
-            sems,
-            sems,
-            sems,
-            sems,
-            pltpu.SemaphoreType.DMA((2,)),
-        ],
-        compiler_params=pltpu.CompilerParams(
-            collective_id=1, has_side_effects=True, vmem_limit_bytes=56 << 20
-        ),
-        name="route",
-    )(target, obs_rows, obs_values)
-
-
-def chain_kernel(
-    high_ref, low_ref, b_ref, start_ref, out_ref,
-    perm, high_got, low_got, b_got, came, went, back, offset, send_sem, recv_sem, tile_send, tile_recv,
-):
-    t, r = lax.axis_index("tm"), lax.axis_index("row")
-    last = lax.axis_size("tm") - 1
-    partner = (t, 1 - r)
-    subs = came.shape[0]
-    width = subs * LANES
-    tile = 256
-    tiles = width // tile
-
-    barrier = pltpu.get_barrier_semaphore()
-
-    def greet(peer):
-        pl.semaphore_signal(barrier, inc=1, device_id=peer, device_id_type=MESH)
-
-    greet(partner)
-
-    @pl.when(t > 0)
-    def _():
-        greet((t - 1, 1))
-
-    @pl.when((r == 1) & (t < last))
-    def _():
-        greet((t + 1, 0))
-        greet((t + 1, 1))
-
-    peers = 1 + jnp.where(t > 0, 1, 0) + jnp.where((r == 1) & (t < last), 2, 0)
-    pl.semaphore_wait(barrier, peers)
+    fetch.wait()
+
+    def divide(k, _):
+        rows = pl.ds(pl.multiple_of(k * LANES, LANES), LANES)
+        high = dynamics[rows, :].astype(jnp.bfloat16)
+        dyn_high[rows, :] = high
+        dyn_low[rows, :] = (dynamics[rows, :] - high.astype(jnp.float32)).astype(jnp.bfloat16)
+        return 0
+
+    lax.fori_loop(0, subs, divide, 0)
+    gain[...] = jnp.zeros_like(gain)
+    moment[...] = jnp.zeros_like(moment)
+
+    chips = block // CAP
+    groups = time_devs // chips
+    nearest = t // chips
+
+    def gather(turn, _):
+        at = jnp.where(nearest * 2 < groups, nearest + turn, nearest + groups - turn)
+        at = lax.rem(at, groups)
+
+        def arrive(source, _):
+            @pl.when(source != me)
+            def _():
+                for copy in copies(source, source):
+                    copy.wait_recv()
+
+            @pl.when(source == me)
+            def _():
+                for copy in keep:
+                    copy.wait()
+
+            return 0
+
+        lax.fori_loop(at * chips * row_devs, (at + 1) * chips * row_devs, arrive, 0)
+        own = pl.ds(pl.multiple_of(at * block, block), block)
+        rows = got[own, :]
+        turned[...] = rows.T
+        tags = jnp.concatenate(
+            [got_values[(at * chips + k) * row_devs][:, :CAP] for k in range(chips)], axis=1
+        )
+        tags = jnp.broadcast_to(tags, (8, block)).astype(jnp.bfloat16)
+        moment[...] += jnp.dot(tags, rows, preferred_element_type=jnp.float32)
+
+        def column(k, _):
+            cols = pl.ds(pl.multiple_of(k * tile, tile), tile)
+            seen = (
+                got[own, cols].astype(jnp.float32)
+                + jnp.dot(got[own, :], dyn_high[:, cols], preferred_element_type=jnp.float32)
+                + jnp.dot(got[own, :], dyn_low[:, cols], preferred_element_type=jnp.float32)
+            )
+            high = seen.astype(jnp.bfloat16)
+            low = (seen - high.astype(jnp.float32)).astype(jnp.bfloat16)
+            gain[:, cols] += jnp.dot(
+                turned[...], high, preferred_element_type=jnp.float32
+            ) + jnp.dot(turned[...], low, preferred_element_type=jnp.float32)
+            return 0
+
+        lax.fori_loop(0, tiles, column, 0)
+        return 0
+
+    lax.fori_loop(0, groups, gather, 0)
 
     def push(source, target, index, peer):
         return pltpu.make_async_remote_copy(
@@ -210,16 +215,35 @@
             for index, (source, target) in enumerate(((high_ref, high_got), (low_ref, low_got)))
         ]
 
+    for sub in range(subs):
+        b_ref[sub : sub + 1, :] = sigma_gain * moment[:1, sub * LANES : (sub + 1) * LANES]
+
     @pl.when(r == 0)
     def _():
         lend.start()
-        for k in range(tiles):
+
+    def settle(k, _):
+        cols = pl.ds(pl.multiple_of(k * tile, tile), tile)
+        for sub in range(subs):
+            own = slice(sub * LANES, (sub + 1) * LANES)
+            diagonal = (
+                lax.broadcasted_iota(jnp.int32, (LANES, tile), 0) + sub * LANES
+                == lax.broadcasted_iota(jnp.int32, (LANES, tile), 1) + k * tile
+            ).astype(jnp.float32)
+            whole = diagonal + dynamics[own, cols] - sigma_gain * gain[own, cols]
+            high = whole.astype(jnp.bfloat16)
+            high_ref[own, cols] = high
+            low_ref[own, cols] = (whole - high.astype(jnp.float32)).astype(jnp.bfloat16)
+            perm[:, sub, cols] = whole
+
+        @pl.when(r == 0)
+        def _():
             for copy in part(k):
                 copy.start()
 
-    for sub in range(subs):
-        own = slice(sub * LANES, (sub + 1) * LANES)
-        perm[:, sub, :] = high_ref[own, :].astype(jnp.float32) + low_ref[own, :].astype(jnp.float32)
+        return 0
+
+    lax.fori_loop(0, tiles, settle, 0)
 
     lane = lax.broadcasted_iota(jnp.int32, (subs, LANES), 1)
     group = 16
@@ -307,69 +331,80 @@
         onward.wait_send()
         aside.wait_send()
 
-
-def run_chain(high, low, offset, initial):
-    width = high.shape[0]
+    def finish(slab, _):
+        @pl.when(slab != me)
+        def _():
+            for copy in copies(slab, slab):
+                copy.wait_send()
+
+        return 0
+
+    lax.fori_loop(0, slabs, finish, 0)
+
+
+def body(initial, dynamics, obs_rows, obs_values, obs_slab):
+    time_devs = lax.axis_size("tm")
+    row_devs = lax.axis_size("row")
+    width = dynamics.shape[1]
+    count, local = obs_rows.shape
+    slabs = time_devs * row_devs
     subs = width // LANES
     tiles = width // 256
     vmem = pl.BlockSpec(memory_space=pltpu.VMEM)
     small = pltpu.VMEM((subs, LANES), jnp.float32)
+    square = pltpu.VMEM((width, width), jnp.bfloat16)
+    square32 = pltpu.VMEM((width, width), jnp.float32)
+    sems = pltpu.SemaphoreType.DMA((slabs,))
     states = pl.pallas_call(
-        chain_kernel,
+        observer_kernel,
         out_shape=jax.ShapeDtypeStruct((2, subs // 2, LANES), jnp.float32),
-        in_specs=[vmem] * 4,
+        in_specs=[vmem, vmem, vmem, pl.BlockSpec(memory_space=pl.ANY), vmem],
         out_specs=vmem,
         scratch_shapes=[
+            pltpu.VMEM((slabs, CAP, local), jnp.bfloat16),
+            pltpu.VMEM((slabs, 1, LANES), jnp.float32),
+            pltpu.VMEM((1, count), jnp.int32),
+            pltpu.VMEM((time_devs * CAP, width), jnp.bfloat16),
+            pltpu.VMEM((slabs, 1, LANES), jnp.float32),
+            square32,
+            square,
+            square,
+            pltpu.VMEM((width, 256), jnp.bfloat16),
+            square32,
+            pltpu.VMEM((8, width), jnp.float32),
+            square,
+            square,
+            small,
             pltpu.VMEM((LANES, subs, width), jnp.float32),
-            pltpu.VMEM((width, width), jnp.bfloat16),
-            pltpu.VMEM((width, width), jnp.bfloat16),
-            small,
-            small,
-            small,
-            small,
-            small,
+            square,
+            square,
+            small,
+            small,
+            small,
+            small,
+            small,
+            sems,
+            sems,
+            sems,
+            sems,
+            pltpu.SemaphoreType.DMA((3,)),
             pltpu.SemaphoreType.DMA((4,)),
             pltpu.SemaphoreType.DMA((3,)),
             pltpu.SemaphoreType.DMA((2, tiles)),
             pltpu.SemaphoreType.DMA((2, tiles)),
         ],
         compiler_params=pltpu.CompilerParams(
-            collective_id=0, has_side_effects=True, vmem_limit_bytes=48 << 20
+            collective_id=0, has_side_effects=True, vmem_limit_bytes=60 << 20
         ),
-        name="chain",
-    )(high, low, offset.reshape(subs, LANES), initial.reshape(subs, LANES))
+        name="observer",
+    )(
+        obs_slab.reshape(1, -1),
+        obs_rows,
+        obs_values.reshape(1, -1),
+        dynamics,
+        initial.reshape(subs, LANES),
+    )
     return states.reshape(2, width // 2)
-
-
-def split(value):
-    high = lax.reduce_precision(value, 8, 7)
-    low = lax.reduce_precision(value - high, 8, 7)
-    return high.astype(jnp.bfloat16), low.astype(jnp.bfloat16)
-
-
-def dot32(left, right, dims):
-    return lax.dot_general(left, right, (dims, ((), ())), preferred_element_type=jnp.float32)
-
-
-def body(initial, dynamics, obs_rows, obs_values, obs_slab):
-    time_devs = lax.axis_size("tm")
-    row_devs = lax.axis_size("row")
-    width = dynamics.shape[1]
-    cols = obs_rows.shape[1]
-    slabs = time_devs * row_devs
-    got, got_values = route(obs_rows, obs_values.reshape(1, -1), obs_slab.reshape(1, -1), slabs)
-    got = got.reshape(time_devs, row_devs, CAP, cols)
-    values = got_values[:, 0, :CAP].astype(jnp.bfloat16).reshape(time_devs, row_devs, CAP)[:, 0].reshape(1, -1)
-    rows = got.transpose(0, 2, 1, 3).reshape(time_devs * CAP, width)
-    high, low = split(dynamics)
-    seen = rows.astype(jnp.float32) + (
-        dot32(rows, high, ((1,), (0,))) + dot32(rows, low, ((1,), (0,)))
-    )
-    seen_high, seen_low = split(seen)
-    gain = dot32(rows, seen_high, ((0,), (0,))) + dot32(rows, seen_low, ((0,), (0,)))
-    transition = jnp.eye(width, dtype=jnp.float32) + dynamics - sigma_gain * gain
-    offset = sigma_gain * dot32(values, rows, ((1,), (0,)))
-    return run_chain(*split(transition), offset, initial)
 
 
 def solution(mesh):

time: 128 us -> 119 us (0.930)
  matrix products: 13.5 us -> 0 us
  Pallas kernels: 108 us -> 116 us
  local copies, waits for them, and re-layouts: 6.36 us -> 2.55 us
    dot_general x5 -> x0, matrix products: 13.5 us -> none  [dot32(): lax.dot_general(left, right, (dims, ((), ())), preferred_element_type=jnp...]
    pallas_call x2 -> x1, Pallas kernels: 108 us -> 116 us  [body(): pl.pallas_call(observer_kernel, out_shape=jax.ShapeDtypeStruct((2, subs /...]
    transpose x1 -> x0, local copies, waits for them, and re-layouts: 3.76 us -> none  [body(): rows = got.transpose(0, 2, 1, 3).reshape(time_devs * CAP, width)]
where the time goes in v3:
time: 119 us; the launch traced here: 118 us
  Pallas kernels  116 us (97%)
  local copies, waits for them, and re-layouts  2.55 us (2%)
    pallas_call x1, Pallas kernels, body(): pl.pallas_call(observer_kernel, out_shape=jax.ShapeDtypeStruct((2, subs /...  116 us

profile of v3, /device:TPU:31, one launch (start us, length us, event | category | flops | bytes accessed | tf_op | source)
XLA Modules:
  0.0 118.4 jit_solution(13902682710842476725)
XLA Ops:
  0.0 1.3 %reshape.13.values_ref = bf16[1,2048]{1,0:T(2,128)(2,1)} reshape(bf16[2048]{0:T(1024)(128)(2,1)} %param.8) | data formatting | bytes 8192 | tf_op jit(solution)/shard_map/reshape | solution.py:403
  1.3 115.9 %observer.1 = f32[2,4,128]{2,1,0:T(4,128)} custom-call(s32[1,2048]{1,0:T(1,128)} %bitcast.7, bf16[2048,512]{1,0:T(8,128)(2,1)} %rows_ref.1, bf16[1,2048]{1,0:T(2,128)(2,1)} %reshape.13.values_ref, f32[1024,1024]{1,0:T(8,128)} %dynamics_ref.1, f32[8,128]{1,0:T(8,128)} %bitcast.8), custom_call_target="tpu_custom_call" | custom-call | tf_op jit(solution)/shard_map/observer/pallas_call | solution.py:358
  117.1 1.3 %copy.8 = f32[1,2,4,128]{3,1,2,0:T(2,128)} copy(f32[1,2,4,128]{3,2,1,0:T(4,128)} %bitcast.6) | data formatting | bytes 8192

commit v4 on v3

--- a/solution.py
+++ b/solution.py
@@ -12,16 +12,30 @@
 sigma_gain = 0.3
 
 
+def chip_at(place):
+    turn = place & 3
+    turn = jnp.where((place >> 2) & 1 == 1, 3 - turn, turn)
+    return (place - (place & 3)) + jnp.where(turn < 2, turn, 5 - turn)
+
+
+def place_of(chip):
+    turn = chip & 3
+    turn = jnp.where(turn < 2, turn, 5 - turn)
+    return (chip - (chip & 3)) + jnp.where((chip >> 2) & 1 == 1, 3 - turn, turn)
+
+
 def observer_kernel(
     target_ref, rows_ref, values_ref, dynamics_ref, start_ref, out_ref,
     sent, sent_values, slot_ref, got, got_values, dynamics, dyn_high, dyn_low, turned, gain, moment,
-    high_ref, low_ref, b_ref, perm, high_got, low_got, b_got, came, went, back, offset,
-    row_send, row_recv, value_send, value_recv, own_sem, send_sem, recv_sem, tile_send, tile_recv,
+    high_ref, low_ref, b_ref, perm, high_got, low_got, b_got, came, went, back, offset, owner_ref,
+    row_send, row_recv, value_send, value_recv, own_sem, send_sem, recv_sem, tile_send, tile_recv, out_send, out_recv,
 ):
     time_devs, row_devs = lax.axis_size("tm"), lax.axis_size("row")
     t, r = lax.axis_index("tm"), lax.axis_index("row")
     slabs = time_devs * row_devs
     last = time_devs - 1
+    place_here = place_of(t)
+    after = chip_at(jnp.minimum(place_here + 1, last))
     me = t * row_devs + r
     partner = (t, 1 - r)
     count, local = rows_ref.shape
@@ -55,8 +69,11 @@
     ).astype(jnp.float32).astype(jnp.bfloat16)
     slab_of = lax.broadcasted_iota(jnp.int32, (slabs, block), 0)
     carry = (slab_of[:, :1] * CAP).astype(jnp.float32)
+    pair = row_devs.bit_length() - 1
+    target = target_ref[...]
+    owner_ref[...] = (chip_at(target >> pair) << pair) + (target & (row_devs - 1))
     for start in range(0, count, block):
-        named = (target_ref[:, start : start + block] == slab_of).astype(jnp.float32)
+        named = (owner_ref[:, start : start + block] == slab_of).astype(jnp.float32)
         ahead = jnp.dot(named.astype(jnp.bfloat16), before, preferred_element_type=jnp.float32)
         slot = jnp.sum(named * (ahead + carry), axis=0, keepdims=True)
         slot_ref[:, start : start + block] = slot.astype(jnp.int32)
@@ -197,11 +214,10 @@
         )
 
     lend = push(b_ref, b_got, 0, partner)
-    answer = push(went, back, 1, partner)
-    onward = push(went, came, 2, (t + 1, 1))
+    onward = push(went, came, 2, (after, 1))
     aside = pltpu.make_async_remote_copy(
         src_ref=went, dst_ref=came, send_sem=send_sem.at[3],
-        recv_sem=recv_sem.at[2], device_id=(t + 1, 0), device_id_type=MESH,
+        recv_sem=recv_sem.at[2], device_id=(after, 0), device_id_type=MESH,
     )
 
     def part(k):
@@ -296,35 +312,56 @@
 
         lax.fori_loop(0, tiles, drain, 0)
 
-    @pl.when(t == 0)
+    @pl.when(place_here == 0)
     def _():
         came[...] = start_ref[...]
 
-    @pl.when(t > 0)
+    @pl.when(place_here > 0)
     def _():
         onward.wait_recv()
 
     went[...] = apply(came[...]) + offset[...]
-    passing = (r == 1) & (t < last)
+    passing = (r == 1) & (place_here < last)
 
     @pl.when(passing)
     def _():
         onward.start()
         aside.start()
 
-    answer.start()
-    answer.wait()
+    stays = place_here == t
+
+    def report(core, sender):
+        return pltpu.make_async_remote_copy(
+            src_ref=went, dst_ref=back.at[sender], send_sem=out_send.at[core],
+            recv_sem=out_recv.at[sender], device_id=(place_here, core), device_id_type=MESH,
+        )
+
+    for core in range(2):
+        @pl.when(jnp.logical_not(stays & (r == core)))
+        def _():
+            report(core, r).start()
+
+        @pl.when(stays & (r == core))
+        def _():
+            back[core] = went[...]
+
+    for core in range(2):
+        @pl.when(jnp.logical_not(stays & (r == core)))
+        def _():
+            report(core, core).wait_recv()
+            report(core, r).wait_send()
+
     half = subs // 2
 
     @pl.when(r == 0)
     def _():
-        out_ref[0] = went[:half, :]
-        out_ref[1] = back[:half, :]
+        out_ref[0] = back[0, :half, :]
+        out_ref[1] = back[1, :half, :]
 
     @pl.when(r == 1)
     def _():
-        out_ref[0] = back[half:, :]
-        out_ref[1] = went[half:, :]
+        out_ref[0] = back[0, half:, :]
+        out_ref[1] = back[1, half:, :]
 
     @pl.when(passing)
     def _():
@@ -381,8 +418,9 @@
             small,
             small,
             small,
+            pltpu.VMEM((2, subs, LANES), jnp.float32),
             small,
-            small,
+            pltpu.VMEM((1, count), jnp.int32),
             sems,
             sems,
             sems,
@@ -392,6 +430,8 @@
             pltpu.SemaphoreType.DMA((3,)),
             pltpu.SemaphoreType.DMA((2, tiles)),
             pltpu.SemaphoreType.DMA((2, tiles)),
+            pltpu.SemaphoreType.DMA((2,)),
+            pltpu.SemaphoreType.DMA((2,)),
         ],
         compiler_params=pltpu.CompilerParams(
             collective_id=0, has_side_effects=True, vmem_limit_bytes=60 << 20

time: 119 us -> 123 us (1.034)
  Pallas kernels: 116 us -> 120 us
    pallas_call x1, Pallas kernels: 116 us -> 120 us  [body(): pl.pallas_call(observer_kernel, out_shape=jax.ShapeDtypeStruct((2, subs /...]
where the time goes in v4:
time: 123 us
  Pallas kernels  120 us (98%)
  local copies, waits for them, and re-layouts  2.55 us (2%)
    pallas_call x1, Pallas kernels, body(): pl.pallas_call(observer_kernel, out_shape=jax.ShapeDtypeStruct((2, subs /...  120 us

profile of v4, /device:TPU:31, one launch (start us, length us, event | category | flops | bytes accessed | tf_op | source)
XLA Modules:
  0.0 123.0 jit_solution(374910132136826005)
XLA Ops:
  0.0 1.3 %reshape.13.values_ref = bf16[1,2048]{1,0:T(2,128)(2,1)} reshape(bf16[2048]{0:T(1024)(128)(2,1)} %param.8) | data formatting | bytes 8192 | tf_op jit(solution)/shard_map/reshape | solution.py:443
  1.3 120.5 %observer.1 = f32[2,4,128]{2,1,0:T(4,128)} custom-call(s32[1,2048]{1,0:T(1,128)} %bitcast.7, bf16[2048,512]{1,0:T(8,128)(2,1)} %rows_ref.1, bf16[1,2048]{1,0:T(2,128)(2,1)} %reshape.13.values_ref, f32[1024,1024]{1,0:T(8,128)} %dynamics_ref.1, f32[8,128]{1,0:T(8,128)} %bitcast.8), custom_call_target="tpu_custom_call" | custom-call | tf_op jit(solution)/shard_map/observer/pallas_call | solution.py:395
  121.7 1.3 %copy.8 = f32[1,2,4,128]{3,1,2,0:T(2,128)} copy(f32[1,2,4,128]{3,2,1,0:T(4,128)} %bitcast.6) | data formatting | bytes 8192

commit v5 on v4

--- a/solution.py
+++ b/solution.py
@@ -10,6 +10,14 @@
 MESH = pl.DeviceIdType.MESH
 
 sigma_gain = 0.3
+
+
+def visit(own, turn, total):
+    if total & (total - 1):
+        return lax.rem(own + turn, total)
+    if total == 4:
+        turn = ((turn & 1) << 1) | (turn >> 1)
+    return own ^ turn
 
 
 def chip_at(place):
@@ -132,12 +140,15 @@
                     copy.start()
 
     mine = me // share
+    layered = 2
     place(mine)
     pl.semaphore_wait(barrier, slabs - 1)
     send(mine)
 
     def step(turn, _):
-        at = lax.rem(mine + turn, blocks)
+        layer, within = turn // layered, lax.rem(turn, layered)
+        at = visit(mine // layered, layer, blocks // layered) * layered
+        at = at + lax.rem(mine + within, layered)
         place(at)
         send(at)
         return 0
@@ -162,8 +173,7 @@
     nearest = t // chips
 
     def gather(turn, _):
-        at = jnp.where(nearest * 2 < groups, nearest + turn, nearest + groups - turn)
-        at = lax.rem(at, groups)
+        at = visit(nearest, turn, groups)
 
         def arrive(source, _):
             @pl.when(source != me)

time: 123 us -> 118 us (0.959)
  Pallas kernels: 120 us -> 115 us
    pallas_call x1, Pallas kernels: 120 us -> 115 us  [body(): pl.pallas_call(observer_kernel, out_shape=jax.ShapeDtypeStruct((2, subs /...]
where the time goes in v5:
time: 118 us
  Pallas kernels  115 us (97%)
  local copies, waits for them, and re-layouts  2.55 us (2%)
    pallas_call x1, Pallas kernels, body(): pl.pallas_call(observer_kernel, out_shape=jax.ShapeDtypeStruct((2, subs /...  115 us

profile of v5, /device:TPU:31, one launch (start us, length us, event | category | flops | bytes accessed | tf_op | source)
XLA Modules:
  0.0 117.9 jit_solution(6208910412570658659)
XLA Ops:
  0.0 1.3 %reshape.13.values_ref = bf16[1,2048]{1,0:T(2,128)(2,1)} reshape(bf16[2048]{0:T(1024)(128)(2,1)} %param.8) | data formatting | bytes 8192 | tf_op jit(solution)/shard_map/reshape | solution.py:453
  1.3 115.3 %observer.1 = f32[2,4,128]{2,1,0:T(4,128)} custom-call(s32[1,2048]{1,0:T(1,128)} %bitcast.7, bf16[2048,512]{1,0:T(8,128)(2,1)} %rows_ref.1, bf16[1,2048]{1,0:T(2,128)(2,1)} %reshape.13.values_ref, f32[1024,1024]{1,0:T(8,128)} %dynamics_ref.1, f32[8,128]{1,0:T(8,128)} %bitcast.8), custom_call_target="tpu_custom_call" | custom-call | tf_op jit(solution)/shard_map/observer/pallas_call | solution.py:405
  116.6 1.3 %copy.8 = f32[1,2,4,128]{3,1,2,0:T(2,128)} copy(f32[1,2,4,128]{3,2,1,0:T(4,128)} %bitcast.6) | data formatting | bytes 8192
